TPU v7x, 256 devices: a whole 4x4x8 slice. The times are simulated.
256 devices in a mesh: frame: 16 (over z_hi, y), space: 16 (over z_lo, x, core).
Axes of the slice: x: 4, y: 4, z: 8 (z_hi: 4, z_lo: 2; z = z_hi * 2 + z_lo), core: 2. Of those that a mesh axis runs over, the one named last changes fastest.
Arguments:
- hidden_in: bfloat16 [2, 16, 32, 64, 1152], P(None, 'frame', 'space'), may hold values from -6 to 6
- attn_cotangent: bfloat16 [2, 16, 32, 64, 1152], P(None, 'frame', 'space'), may hold values from -6 to 6
- w_qkv: bfloat16 [1152, 3456], P('space'), may hold values from -0.1875 to 0.1875
- modulation_table: bfloat16 [1000, 2, 1152], replicated, may hold values from -3 to 3
- snr_table: float32 [1000], replicated, may hold values from 0.1 to 1
- timestep: int32 [2], replicated, may hold values from 0 to 999
- weight_index: int32 [2], replicated, may hold values from 0 to 999
Outputs:
- grad_input: bfloat16 [2, 16, 32, 64, 1152], P(None, 'frame', 'space')
- grad_w_qkv: float32 [1152, 3456], P('space')
- grad_modulation: float32 [2, 2, 1152], replicated
All inputs are finite; a program needn't handle non-finite values.
Results may differ from a plain program's by a relative error of at most 0.029.
Values may be sent and summed in bfloat16 or wider, within the bound.
A program may use at most 128 MiB of HBM per device.

v0:
```python
import jax
import jax.numpy as jnp
from jax import lax
from jax.sharding import PartitionSpec as P

HEADS = 16
HEAD_DIM = 72


def attend_back(queries, keys, values, upstream):
    factor = queries.shape[-1] ** (-0.5)
    queries = queries.astype(jnp.float32)
    keys = keys.astype(jnp.float32)
    values = values.astype(jnp.float32)
    upstream = upstream.astype(jnp.float32)
    highest = lax.Precision.HIGHEST
    scores = jnp.einsum("bfxhe,bgxhe->bxhfg", queries, keys, precision=highest) * factor
    expd = jnp.exp(scores)
    probs = expd / jnp.sum(expd, axis=-1, keepdims=True)
    grad_probs = jnp.einsum("bfxhe,bgxhe->bxhfg", upstream, values, precision=highest)
    grad_values = jnp.einsum("bxhfg,bfxhe->bgxhe", probs, upstream, precision=highest)
    grad_scores = probs * (grad_probs - jnp.sum(probs * grad_probs, axis=-1, keepdims=True))
    grad_queries = jnp.einsum("bxhfg,bgxhe->bfxhe", grad_scores, keys, precision=highest) * factor
    grad_keys = jnp.einsum("bxhfg,bfxhe->bgxhe", grad_scores, queries, precision=highest) * factor
    return (
        grad_queries.astype(jnp.bfloat16),
        grad_keys.astype(jnp.bfloat16),
        grad_values.astype(jnp.bfloat16),
    )


def per_device(
    hidden_in, attn_cotangent, w_qkv, modulation_table, snr_table, timestep, weight_index
):
    clip_count, frame_dev, row_dev, col_count, model_width = hidden_in.shape
    frame_n = lax.axis_size("frame")
    space_n = lax.axis_size("space")
    positions = row_dev * col_count
    w_full = lax.all_gather(w_qkv, "space", axis=0, tiled=True)
    both = jnp.stack(
        [
            hidden_in.reshape(clip_count, frame_dev, positions, model_width),
            attn_cotangent.reshape(clip_count, frame_dev, positions, model_width),
        ],
        axis=3,
    )
    both = lax.all_to_all(both, "frame", split_axis=2, concat_axis=1, tiled=True)
    frames = both.shape[1]
    across = both.shape[2]
    values_in = both[:, :, :, 0].astype(jnp.float32)
    average = jnp.mean(values_in, axis=-1, keepdims=True)
    centered = values_in - average
    variance = jnp.mean(centered * centered, axis=-1, keepdims=True)
    inverse_std = lax.rsqrt(variance + 1e-06)
    normed = centered * inverse_std
    modulation = modulation_table[timestep].astype(jnp.float32)
    shift = modulation[:, 0][:, None, None, :]
    scale = modulation[:, 1][:, None, None, :]
    modulated = (normed * (1.0 + scale) + shift).astype(jnp.bfloat16)
    mod_rows = modulated.reshape(-1, model_width)
    projected = jnp.dot(mod_rows, w_full, preferred_element_type=jnp.float32).astype(jnp.bfloat16)
    pieces = projected.reshape(clip_count, frames, across, 3, HEADS, HEAD_DIM)
    loss_weight = snr_table[weight_index]
    upstream = (loss_weight[:, None, None, None] * both[:, :, :, 1].astype(jnp.float32)).astype(
        jnp.bfloat16
    )
    upstream = upstream.reshape(clip_count, frames, across, HEADS, HEAD_DIM)
    head_grads = attend_back(pieces[:, :, :, 0], pieces[:, :, :, 1], pieces[:, :, :, 2], upstream)
    grad_rows = jnp.stack(head_grads, axis=3).reshape(-1, 3 * model_width)
    grad_scale_factor = float(mod_rows.shape[0] * frame_n * space_n) ** (-0.5)
    term = lax.dot_general(
        mod_rows, grad_rows, (((0,), (0,)), ((), ())), preferred_element_type=jnp.float32
    ).astype(jnp.bfloat16)
    col_blk = 3 * model_width // frame_n
    share = lax.psum_scatter(term, "space", scatter_dimension=0, tiled=True)
    share = share.reshape(share.shape[0], frame_n, col_blk)
    share = lax.psum_scatter(share, "frame", scatter_dimension=1, tiled=True)
    grad_weight = lax.all_gather(share, "frame", axis=1, tiled=True)
    grad_weight = grad_weight.reshape(share.shape[0], 3 * model_width)
    grad_weight = grad_weight.astype(jnp.float32) * grad_scale_factor
    grad_hidden = lax.dot_general(
        grad_rows, w_full, (((1,), (1,)), ((), ())), preferred_element_type=jnp.float32
    )
    grad_hidden = grad_hidden.reshape(values_in.shape)
    local_sums = jnp.stack(
        [jnp.sum(grad_hidden, axis=(1, 2)), jnp.sum(grad_hidden * normed, axis=(1, 2))], axis=1
    )
    grad_modulation = lax.psum(local_sums, ("frame", "space")) * grad_scale_factor
    grad_normed = grad_hidden * (1.0 + scale)
    grad_input = (
        grad_normed
        - jnp.mean(grad_normed, axis=-1, keepdims=True)
        - normed * jnp.mean(grad_normed * normed, axis=-1, keepdims=True)
    ) * inverse_std
    grad_input = grad_input.astype(jnp.bfloat16)
    grad_input = lax.all_to_all(grad_input, "frame", split_axis=1, concat_axis=2, tiled=True)
    grad_input = grad_input.reshape(clip_count, frame_dev, row_dev, col_count, model_width)
    return (grad_input, grad_weight, grad_modulation)


def solution(mesh):
    in_specs = (
        P(None, "frame", "space", None, None),
        P(None, "frame", "space", None, None),
        P("space", None),
        P(),
        P(),
        P(),
        P(),
    )
    out_specs = (P(None, "frame", "space", None, None), P("space", None), P())
    return jax.shard_map(
        per_device, mesh=mesh, in_specs=in_specs, out_specs=out_specs, check_vma=False
    )
```

profile of v0, /device:TPU:2, one launch (start us, length us, event | category | flops | bytes accessed | tf_op | source)
XLA Modules:
  0.0 375.7 jit_solution(3701805909269728193)
XLA Ops:
  7.2 0.7 all-gather.2.cloned.1.call-update
  7.9 1.7 copy.38
  9.6 1.7 copy.39
  11.3 2.7 pad_maximum_fusion.1
  13.9 11.2 %all-to-all-start = ((bf16[2,1,128,2,1152]{4,0,3,1,2:T(2,128)(2,1)}), bf16[2,1,128,2,1152]{4,0,3,1,2:T(2,128)(2,1)S(1)}, u32[]{:S(2)}, u32[]{:S(2)}) async-start(bf16[2,1,128,2,1152]{4,0,3,1,2:T(2,128)(2,1)} %pad_maximum_fusion.1), calls=%async_computation | async-start | bytes 2359296 | tf_op jit(solution)/shard_map/all_to_all | solution.py:47
  25.2 0.0 reduce-scatter.8.cloned.1.call-start
  25.2 2.9 gather_fusion
  28.2 0.6 gather_fusion.1
  28.9 26.7 %all-to-all-done = bf16[2,1,128,2,1152]{4,0,3,1,2:T(2,128)(2,1)S(1)} async-done(((bf16[2,1,128,2,1152]{4,0,3,1,2:T(2,128)(2,1)}), bf16[2,1,128,2,1152]{4,0,3,1,2:T(2,128)(2,1)S(1)}, u32[]{:S(2)}, u32[]{:S(2)}) %all-to-all-start) | async-done | bytes 1179680 | tf_op jit(solution)/shard_map/all_to_all | solution.py:47
  55.5 0.1 copy.85
  55.7 0.2 convert_reduce_fusion
  55.8 0.1 div.23
  55.9 0.3 multiply_reduce_fusion.3
  56.2 0.1 rsqrt.13
  56.3 0.1 slice_convert_fusion
  56.4 3.1 reshape.157
  59.6 0.3 fusion.8
  59.9 28.9 %all-gather.2.cloned.1.call-done = bf16[1152,3456]{1,0:T(8,128)(2,1)} async-done(((bf16[72,3456]{1,0:T(8,128)(2,1)}), bf16[1152,3456]{1,0:T(8,128)(2,1)}) %all-gather.2.cloned.1.call-update) | async-done | bytes 7962640 | tf_op jit(solution)/shard_map/all_gather | solution.py:39
  88.8 7.0 %convolution_convert_fusion.1 = bf16[256,3456]{1,0:T(8,128)(2,1)} fusion(bf16[256,1152]{1,0:T(8,128)(2,1)S(1)} %fusion.8, bf16[1152,3456]{1,0:T(8,128)(2,1)} %all-gather.2.cloned.1.call-done), kind=kOutput, calls=%fused_computation.5 | convolution fusion | flops 2039316480 | bytes 10321920 | tf_op jit(solution)/shard_map/dot_general | solution.py:61
  95.8 7.1 %reshape.152 = bf16[2,16,8,3,16,72]{5,4,3,2,1,0:T(8,128)(2,1)S(1)} reshape(bf16[256,3456]{1,0:T(8,128)(2,1)} %convolution_convert_fusion.1) | data formatting | bytes 3538944 | tf_op jit(solution)/shard_map/reshape | solution.py:62
  102.9 0.9 fusion.18
  103.9 1.7 fusion.4
  105.6 2.3 multiply_reduce_fusion
  107.9 2.4 fusion.6
  110.3 2.2 fusion.7
  112.6 2.8 fusion.5
  115.3 0.8 pad_maximum_fusion
  116.1 0.8 copy.46
  116.9 4.6 %dot_general.32 = bf16[2,16,8,3456]{3,2,1,0:T(8,128)(2,1)} reshape(bf16[2,16,8,3,16,72]{5,4,3,2,1,0:T(8,128)(2,1)S(1)} %copy.46) | data formatting | bytes 3538944 | tf_op jit(solution)/shard_map/dot_general | solution.py:81
  121.5 4.6 %reshape.154 = bf16[256,3456]{1,0:T(8,128)(2,1)} reshape(bf16[2,16,8,3,16,72]{5,4,3,2,1,0:T(8,128)(2,1)S(1)} %copy.46) | data formatting | bytes 3538944 | tf_op jit(solution)/shard_map/reshape | solution.py:69
  126.1 6.7 %multiply_reduce_fusion.1 = (f32[2,1152]{1,0:T(2,128)S(1)}, f32[2,16,8]{2,1,0:T(8,128)S(1)}, f32[2,16,8]{2,1,0:T(8,128)S(1)}, f32[2,1152]{1,0:T(2,128)S(1)}, bf1...) fusion(f32[2,16,8]{2,1,0:T(8,128)S(1)} %add_rsqrt_fusion, ...), kind=kOutput, calls=%fused_computation.28 | convolution fusion | flops 2042260480 | bytes 12132352 | tf_op jit(solution)/shard_map/dot_general | solution.py:81
  132.8 5.4 %convolution_convert_fusion = bf16[1152,3456]{1,0:T(8,128)(2,1)} fusion(bf16[256,1152]{1,0:T(8,128)(2,1)S(1)} %bitcast.101, bf16[256,3456]{1,0:T(8,128)(2,1)S(1)} %copy-done.3), kind=kOutput, calls=%fused_computation.2 | convolution fusion | flops 2042413056 | bytes 10321920 | tf_op jit(solution)/shard_map/dot_general | solution.py:71
  138.3 1.2 copy-done.2
  139.5 0.4 multiply_convert_fusion.2
  140.0 0.9 copy.47
  140.8 8.8 %all-to-all-start.1 = ((bf16[2,16,8,1152]{3,2,0,1:T(8,128)(2,1)}), bf16[2,16,8,1152]{3,2,0,1:T(8,128)(2,1)S(1)}, u32[]{:S(2)}, u32[]{:S(2)}) async-start(bf16[2,16,8,1152]{3,2,0,1:T(8,128)(2,1)} %copy.47), calls=%async_computation.1 | async-start | bytes 1179648 | tf_op jit(solution)/shard_map/all_to_all | solution.py:96
  149.6 0.0 reduce-scatter.6.cloned.1.call-start
  149.7 76.9 %reduce-scatter.8.cloned.1.call-done = bf16[72,3456]{1,0:T(8,128)(2,1)} async-done(((bf16[1152,3456]{1,0:T(8,128)(2,1)}), bf16[72,3456]{1,0:T(8,128)(2,1)}) %reduce-scatter.8.cloned.1.call-update) | async-done | bytes 497680
  226.6 2.8 reshape.155
  229.3 1.0 copy.50
  230.4 80.8 %psum.7 = f32[2,2,1152]{2,0,1:T(2,128)S(1)} all-reduce(f32[2,2,1152]{2,0,1:T(2,128)S(1)} %pad_maximum_fusion.2), channel_id=1, replica_groups=mesh['frame'=16,'space'=16] {'frame','space'}, use_global_device_ids=true, to_apply=%region_10.0 | all-reduce | flops 4608 | bytes 36864 | tf_op jit(solution)/shard_map/psum | solution.py:88
  311.2 0.6 copy.53
  311.8 0.9 copy.48
  312.6 8.1 %reduce-scatter.6.cloned.1.call-done = bf16[72,1,216]{2,0,1:T(8,128)(2,1)} async-done(((bf16[72,16,216]{2,0,1:T(8,128)(2,1)}), bf16[72,1,216]{2,0,1:T(8,128)(2,1)}) %reduce-scatter.6.cloned.1.call-update) | async-done | bytes 31120 | tf_op jit(solution)/shard_map/reduce_scatter | solution.py:77
  320.8 46.3 %all_gather.7 = bf16[72,16,216]{2,0,1:T(8,128)(2,1)S(1)} all-gather(bf16[72,1,216]{2,0,1:T(8,128)(2,1)} %reduce-scatter.6.cloned.1.call-done), channel_id=1, replica_groups=mesh['frame'=16,'space'=16] {'frame'}, dimensions={1}, use_global_device_ids=true | all-gather | bytes 528768 | tf_op jit(solution)/shard_map/all_gather | solution.py:78
  367.0 0.1 convert_multiply_fusion
  367.1 0.4 copy.51
  367.5 1.6 mul.137
  (31 shorter events, 0.2 us)
Async XLA Ops:
  7.2 21.0 %copy-start = (f32[1000]{0:T(1024)S(1)}, f32[1000]{0:T(1024)}, u32[]{:S(2)}) copy-start(f32[1000]{0:T(1024)} %param.11) | copy-start | bytes 12004
  7.2 81.6 %all-gather.2.cloned.1.call-start = ((), (), s32[]{:S(2)}) async-start(), calls=%async_computation.4 | async-start | bytes 8460288 | tf_op jit(solution)/shard_map/all_gather | solution.py:39
  11.3 13.9 %copy-start.5 = (s32[2]{0:T(128)S(1)}, s32[2]{0:T(128)}, u32[]{:S(2)}) copy-start(s32[2]{0:T(128)} %param.12) | copy-start | bytes 28
  11.3 16.9 %copy-start.6 = (s32[2]{0:T(128)S(1)}, s32[2]{0:T(128)}, u32[]{:S(2)}) copy-start(s32[2]{0:T(128)} %param.13) | copy-start | bytes 28
  13.9 41.6 %all-to-all-start = ((bf16[2,1,128,2,1152]{4,0,3,1,2:T(2,128)(2,1)}), bf16[2,1,128,2,1152]{4,0,3,1,2:T(2,128)(2,1)S(1)}, u32[]{:S(2)}, u32[]{:S(2)}) async-start(bf16[2,1,128,2,1152]{4,0,3,1,2:T(2,128)(2,1)} %pad_maximum_fusion.1), calls=%async_computation | async-start | bytes 2359296 | tf_op jit(solution)/shard_map/all_to_all | solution.py:47
  25.2 201.4 %reduce-scatter.8.cloned.1.call-start = ((), (), s32[]{:S(2)}) async-start(), calls=%async_computation.6 | async-start | bytes 8460288
  55.7 3.9 %copy-start.1 = (bf16[2,1,128,2,1152]{4,2,0,3,1:T(8,128)(2,1)}, bf16[2,1,128,2,1152]{4,2,0,3,1:T(8,128)(2,1)S(1)}, u32[]{:S(2)}) copy-start(bf16[2,1,128,2,1152]{4,2,0,3,1:T(8,128)(2,1)S(1)} %copy.85) | copy-start | bytes 3538948
  103.9 1.7 copy-start.4
  126.1 6.7 %copy-start.3 = (bf16[256,3456]{1,0:T(8,128)(2,1)S(1)}, bf16[256,3456]{1,0:T(8,128)(2,1)}, u32[]{:S(2)}) copy-start(bf16[256,3456]{1,0:T(8,128)(2,1)} %reshape.154) | copy-start | bytes 5308420
  138.3 1.3 copy-start.2
  140.8 170.9 %all-to-all-start.1 = ((bf16[2,16,8,1152]{3,2,0,1:T(8,128)(2,1)}), bf16[2,16,8,1152]{3,2,0,1:T(8,128)(2,1)S(1)}, u32[]{:S(2)}, u32[]{:S(2)}) async-start(bf16[2,16,8,1152]{3,2,0,1:T(8,128)(2,1)} %copy.47), calls=%async_computation.1 | async-start | bytes 1179648 | tf_op jit(solution)/shard_map/all_to_all | solution.py:96
  149.6 171.1 %reduce-scatter.6.cloned.1.call-start = ((), (), s32[]{:S(2)}) async-start(), calls=%async_computation.5 | async-start | bytes 626688 | tf_op jit(solution)/shard_map/reduce_scatter | solution.py:77
Sparse Core Ops, SparseCore 0:
  9.9 78.8 all-gather.1
  138.4 88.0 reduce-scatter.7
  230.6 90.0 reduce-scatter.5
where the time goes:
time: 376 us
  waiting for transfers between devices  141 us (38%)
  blocking collectives  127 us (34%)
  local copies, waits for them, and re-layouts  37.7 us (10%)
  matrix products  30.6 us (8%)
  starting transfers between devices  20.1 us (5%)
  between operations  14.1 us (4%)
  other arithmetic  4.83 us (1%)
    psum x1, blocking collectives, per_device(): lax.psum(local_sums, ('frame', 'space')) * grad_scale_factor  80.8 us
    unnamed x4, waiting for transfers between devices  77.6 us
    all_gather x1, blocking collectives, per_device(): grad_weight = lax.all_gather(share, 'frame', axis=1, tiled=True)  46.3 us
    all_gather x1, waiting for transfers between devices, per_device(): w_full = lax.all_gather(w_qkv, 'space', axis=0, tiled=True)  28.9 us
    all_to_all x1, waiting for transfers between devices, per_device(): lax.all_to_all(both, 'frame', split_axis=2, concat_axis=1, tiled=True)  26.7 us
    all_to_all x1, starting transfers between devices, per_device(): lax.all_to_all(both, 'frame', split_axis=2, concat_axis=1, tiled=True)  11.2 us
    all_to_all x1, starting transfers between devices, per_device(): lax.all_to_all(grad_input, 'frame', split_axis=1, concat_axis=2, tiled=True)  8.77 us
    reduce_scatter x1, waiting for transfers between devices, per_device(): share = lax.psum_scatter(share, 'frame', scatter_dimension=1, tiled=True)  8.13 us
  transfers between devices with their start and end apart: 5, of which 4 were waited for; matrix products, arithmetic and copies ran while one was open for 5% of the time, Pallas kernels for 0%

commit v1 on v0

--- a/solution.py
+++ b/solution.py
@@ -75,7 +75,8 @@
     share = lax.psum_scatter(term, "space", scatter_dimension=0, tiled=True)
     share = share.reshape(share.shape[0], frame_n, col_blk)
     share = lax.psum_scatter(share, "frame", scatter_dimension=1, tiled=True)
-    grad_weight = lax.all_gather(share, "frame", axis=1, tiled=True)
+    sent = jnp.stack([share] * lax.axis_size("frame"))
+    grad_weight = jnp.concatenate(lax.all_to_all(sent, "frame", 0, 0), axis=1)
     grad_weight = grad_weight.reshape(share.shape[0], 3 * model_width)
     grad_weight = grad_weight.astype(jnp.float32) * grad_scale_factor
     grad_hidden = lax.dot_general(

time: 376 us -> 417 us (1.11)
  waiting for transfers between devices: 141 us -> 224 us
  blocking collectives: 127 us -> 76.5 us
  starting transfers between devices: 20.1 us -> 25.9 us
    reduce_scatter x1, waiting for transfers between devices: 8.13 us -> 90.4 us  [per_device(): share = lax.psum_scatter(share, 'frame', scatter_dimension=1, tiled=True)]
    all_gather x1 -> x0, blocking collectives: 46.3 us -> none  [per_device(): grad_weight = lax.all_gather(share, 'frame', axis=1, tiled=True)]
    all_to_all x0 -> x1, starting transfers between devices: none -> 5.85 us  [per_device(): grad_weight = jnp.concatenate(lax.all_to_all(sent, 'frame', 0, 0), axis=1)]
    psum x1, blocking collectives: 80.8 us -> 76.5 us  [per_device(): lax.psum(local_sums, ('frame', 'space')) * grad_scale_factor]
  transfers between devices with their start and end apart: 5 -> 6, of which waited for: 4 -> 4; matrix products, arithmetic and copies ran while one was open for 5% -> 5% of each run, Pallas kernels for 0% -> 0%
where the time goes in v1:
time: 417 us; the launch traced here: 415 us
  waiting for transfers between devices  224 us (54%)
  blocking collectives  76.5 us (18%)
  local copies, waits for them, and re-layouts  39.4 us (9%)
  matrix products  30.6 us (7%)
  starting transfers between devices  25.9 us (6%)
  between operations  14.1 us (3%)
  other arithmetic  4.83 us (1%)
    reduce_scatter x1, waiting for transfers between devices, per_device(): share = lax.psum_scatter(share, 'frame', scatter_dimension=1, tiled=True)  90.4 us
    unnamed x4, waiting for transfers between devices  77.6 us
    psum x1, blocking collectives, per_device(): lax.psum(local_sums, ('frame', 'space')) * grad_scale_factor  76.5 us
    all_gather x1, waiting for transfers between devices, per_device(): w_full = lax.all_gather(w_qkv, 'space', axis=0, tiled=True)  28.9 us
    all_to_all x1, waiting for transfers between devices, per_device(): lax.all_to_all(both, 'frame', split_axis=2, concat_axis=1, tiled=True)  26.7 us
    all_to_all x1, starting transfers between devices, per_device(): lax.all_to_all(both, 'frame', split_axis=2, concat_axis=1, tiled=True)  11.2 us
    all_to_all x1, starting transfers between devices, per_device(): lax.all_to_all(grad_input, 'frame', split_axis=1, concat_axis=2, tiled=True)  8.77 us
  transfers between devices with their start and end apart: 6, of which 4 were waited for; matrix products, arithmetic and copies ran while one was open for 5% of the time, Pallas kernels for 0%

profile of v1, /device:TPU:2, one launch (start us, length us, event | category | flops | bytes accessed | tf_op | source)
XLA Modules:
  0.0 414.9 jit_solution(17517000707990849442)
XLA Ops:
  7.2 0.7 all-gather.2.cloned.1.call-update
  7.9 1.7 copy.53
  9.6 1.7 copy.54
  11.3 2.7 pad_maximum_fusion.1
  13.9 11.2 %all-to-all-start = ((bf16[2,1,128,2,1152]{4,0,3,1,2:T(2,128)(2,1)}), bf16[2,1,128,2,1152]{4,0,3,1,2:T(2,128)(2,1)S(1)}, u32[]{:S(2)}, u32[]{:S(2)}) async-start(bf16[2,1,128,2,1152]{4,0,3,1,2:T(2,128)(2,1)} %pad_maximum_fusion.1), calls=%async_computation | async-start | bytes 2359296 | tf_op jit(solution)/shard_map/all_to_all | solution.py:47
  25.2 0.0 reduce-scatter.8.cloned.1.call-start
  25.2 2.9 gather_fusion
  28.2 0.6 gather_fusion.1
  28.9 26.7 %all-to-all-done = bf16[2,1,128,2,1152]{4,0,3,1,2:T(2,128)(2,1)S(1)} async-done(((bf16[2,1,128,2,1152]{4,0,3,1,2:T(2,128)(2,1)}), bf16[2,1,128,2,1152]{4,0,3,1,2:T(2,128)(2,1)S(1)}, u32[]{:S(2)}, u32[]{:S(2)}) %all-to-all-start) | async-done | bytes 1179680 | tf_op jit(solution)/shard_map/all_to_all | solution.py:47
  55.5 0.1 copy.100
  55.7 0.2 convert_reduce_fusion
  55.8 0.1 div.23
  55.9 0.3 multiply_reduce_fusion.3
  56.2 0.1 rsqrt.13
  56.3 0.1 slice_convert_fusion
  56.4 3.1 reshape.160
  59.6 0.3 fusion.8
  59.9 28.9 %all-gather.2.cloned.1.call-done = bf16[1152,3456]{1,0:T(8,128)(2,1)} async-done(((bf16[72,3456]{1,0:T(8,128)(2,1)}), bf16[1152,3456]{1,0:T(8,128)(2,1)}) %all-gather.2.cloned.1.call-update) | async-done | bytes 7962640 | tf_op jit(solution)/shard_map/all_gather | solution.py:39
  88.8 7.0 %convolution_convert_fusion.1 = bf16[256,3456]{1,0:T(8,128)(2,1)} fusion(bf16[256,1152]{1,0:T(8,128)(2,1)S(1)} %fusion.8, bf16[1152,3456]{1,0:T(8,128)(2,1)} %all-gather.2.cloned.1.call-done), kind=kOutput, calls=%fused_computation.5 | convolution fusion | flops 2039316480 | bytes 10321920 | tf_op jit(solution)/shard_map/dot_general | solution.py:61
  95.8 7.1 %reshape.155 = bf16[2,16,8,3,16,72]{5,4,3,2,1,0:T(8,128)(2,1)S(1)} reshape(bf16[256,3456]{1,0:T(8,128)(2,1)} %convolution_convert_fusion.1) | data formatting | bytes 3538944 | tf_op jit(solution)/shard_map/reshape | solution.py:62
  102.9 0.9 fusion.18
  103.9 1.7 fusion.4
  105.6 2.3 multiply_reduce_fusion
  107.9 2.4 fusion.6
  110.3 2.2 fusion.7
  112.6 2.8 fusion.5
  115.3 0.8 pad_maximum_fusion
  116.1 0.8 copy.61
  116.9 4.6 %dot_general.32 = bf16[2,16,8,3456]{3,2,1,0:T(8,128)(2,1)} reshape(bf16[2,16,8,3,16,72]{5,4,3,2,1,0:T(8,128)(2,1)S(1)} %copy.61) | data formatting | bytes 3538944 | tf_op jit(solution)/shard_map/dot_general | solution.py:82
  121.5 4.6 %reshape.157 = bf16[256,3456]{1,0:T(8,128)(2,1)} reshape(bf16[2,16,8,3,16,72]{5,4,3,2,1,0:T(8,128)(2,1)S(1)} %copy.61) | data formatting | bytes 3538944 | tf_op jit(solution)/shard_map/reshape | solution.py:69
  126.1 6.7 %multiply_reduce_fusion.1 = (f32[2,1152]{1,0:T(2,128)S(1)}, f32[2,16,8]{2,1,0:T(8,128)S(1)}, f32[2,16,8]{2,1,0:T(8,128)S(1)}, f32[2,1152]{1,0:T(2,128)S(1)}, bf1...) fusion(f32[2,16,8]{2,1,0:T(8,128)S(1)} %add_rsqrt_fusion, ...), kind=kOutput, calls=%fused_computation.28 | convolution fusion | flops 2042260480 | bytes 12132352 | tf_op jit(solution)/shard_map/dot_general | solution.py:82
  132.8 5.4 %convolution_convert_fusion = bf16[1152,3456]{1,0:T(8,128)(2,1)} fusion(bf16[256,1152]{1,0:T(8,128)(2,1)S(1)} %bitcast.108, bf16[256,3456]{1,0:T(8,128)(2,1)S(1)} %copy-done.3), kind=kOutput, calls=%fused_computation.2 | convolution fusion | flops 2042413056 | bytes 10321920 | tf_op jit(solution)/shard_map/dot_general | solution.py:71
  138.3 1.2 copy-done.2
  139.5 0.4 multiply_convert_fusion.2
  140.0 0.9 copy.62
  140.8 8.8 %all-to-all-start.1 = ((bf16[2,16,8,1152]{3,2,0,1:T(8,128)(2,1)}), bf16[2,16,8,1152]{3,2,0,1:T(8,128)(2,1)S(1)}, u32[]{:S(2)}, u32[]{:S(2)}) async-start(bf16[2,16,8,1152]{3,2,0,1:T(8,128)(2,1)} %copy.62), calls=%async_computation.1 | async-start | bytes 1179648 | tf_op jit(solution)/shard_map/all_to_all | solution.py:97
  149.7 76.9 %reduce-scatter.8.cloned.1.call-done = bf16[72,3456]{1,0:T(8,128)(2,1)} async-done(((bf16[1152,3456]{1,0:T(8,128)(2,1)}), bf16[72,3456]{1,0:T(8,128)(2,1)}) %reduce-scatter.8.cloned.1.call-update) | async-done | bytes 497680
  226.6 2.8 reshape.158
  229.3 1.0 copy.65
  230.4 90.4 %reduce-scatter.6.cloned.1.call-done = bf16[72,1,216]{2,0,1:T(8,128)(2,1)} async-done(((bf16[72,16,216]{2,0,1:T(8,128)(2,1)}), bf16[72,1,216]{2,0,1:T(8,128)(2,1)}) %reduce-scatter.6.cloned.1.call-update) | async-done | bytes 31120 | tf_op jit(solution)/shard_map/reduce_scatter | solution.py:77
  320.8 1.6 stack.23
  322.4 5.9 %all-to-all-start.2 = ((bf16[16,72,1,216]{3,1,2,0:T(8,128)(2,1)}), bf16[16,72,1,216]{3,1,2,0:T(8,128)(2,1)S(1)}, u32[]{:S(2)}, u32[]{:S(2)}) async-start(bf16[16,72,1,216]{3,1,2,0:T(8,128)(2,1)} %stack.23), calls=%async_computation.3 | async-start | bytes 1179648 | tf_op jit(solution)/shard_map/all_to_all | solution.py:79
  328.3 76.5 %psum.7 = f32[2,2,1152]{2,0,1:T(2,128)S(1)} all-reduce(f32[2,2,1152]{2,0,1:T(2,128)S(1)} %pad_maximum_fusion.2), channel_id=1, replica_groups=mesh['frame'=16,'space'=16] {'frame','space'}, use_global_device_ids=true, to_apply=%region_10.0 | all-reduce | flops 4608 | bytes 36864 | tf_op jit(solution)/shard_map/psum | solution.py:89
  404.8 0.6 copy.68
  405.4 0.9 copy.63
  406.3 0.1 multiply_bitcast_fusion
  406.3 0.4 copy.66
  406.7 1.6 mul.141
  (33 shorter events, 0.3 us)
Async XLA Ops:
  7.2 21.0 %copy-start = (f32[1000]{0:T(1024)S(1)}, f32[1000]{0:T(1024)}, u32[]{:S(2)}) copy-start(f32[1000]{0:T(1024)} %param.11) | copy-start | bytes 12004
  7.2 81.6 %all-gather.2.cloned.1.call-start = ((), (), s32[]{:S(2)}) async-start(), calls=%async_computation.5 | async-start | bytes 8460288 | tf_op jit(solution)/shard_map/all_gather | solution.py:39
  11.3 13.9 %copy-start.5 = (s32[2]{0:T(128)S(1)}, s32[2]{0:T(128)}, u32[]{:S(2)}) copy-start(s32[2]{0:T(128)} %param.12) | copy-start | bytes 28
  11.3 16.9 %copy-start.6 = (s32[2]{0:T(128)S(1)}, s32[2]{0:T(128)}, u32[]{:S(2)}) copy-start(s32[2]{0:T(128)} %param.13) | copy-start | bytes 28
  13.9 41.6 %all-to-all-start = ((bf16[2,1,128,2,1152]{4,0,3,1,2:T(2,128)(2,1)}), bf16[2,1,128,2,1152]{4,0,3,1,2:T(2,128)(2,1)S(1)}, u32[]{:S(2)}, u32[]{:S(2)}) async-start(bf16[2,1,128,2,1152]{4,0,3,1,2:T(2,128)(2,1)} %pad_maximum_fusion.1), calls=%async_computation | async-start | bytes 2359296 | tf_op jit(solution)/shard_map/all_to_all | solution.py:47
  25.2 201.4 %reduce-scatter.8.cloned.1.call-start = ((), (), s32[]{:S(2)}) async-start(), calls=%async_computation.7 | async-start | bytes 8460288
  55.7 3.9 copy-start.1
  103.9 1.7 copy-start.4
  126.1 6.7 %copy-start.3 = (bf16[256,3456]{1,0:T(8,128)(2,1)S(1)}, bf16[256,3456]{1,0:T(8,128)(2,1)}, u32[]{:S(2)}) copy-start(bf16[256,3456]{1,0:T(8,128)(2,1)} %reshape.157) | copy-start | bytes 5308420
  138.3 1.3 copy-start.2
  140.8 89.5 %all-to-all-start.1 = ((bf16[2,16,8,1152]{3,2,0,1:T(8,128)(2,1)}), bf16[2,16,8,1152]{3,2,0,1:T(8,128)(2,1)S(1)}, u32[]{:S(2)}, u32[]{:S(2)}) async-start(bf16[2,16,8,1152]{3,2,0,1:T(8,128)(2,1)} %copy.62), calls=%async_computation.1 | async-start | bytes 1179648 | tf_op jit(solution)/shard_map/all_to_all | solution.py:97
  149.6 171.1 %reduce-scatter.6.cloned.1.call-start = ((), (), s32[]{:S(2)}) async-start(), calls=%async_computation.6 | async-start | bytes 626688 | tf_op jit(solution)/shard_map/reduce_scatter | solution.py:77
  322.4 83.9 %all-to-all-start.2 = ((bf16[16,72,1,216]{3,1,2,0:T(8,128)(2,1)}), bf16[16,72,1,216]{3,1,2,0:T(8,128)(2,1)S(1)}, u32[]{:S(2)}, u32[]{:S(2)}) async-start(bf16[16,72,1,216]{3,1,2,0:T(8,128)(2,1)} %stack.23), calls=%async_computation.3 | async-start | bytes 1179648 | tf_op jit(solution)/shard_map/all_to_all | solution.py:79
Sparse Core Ops, SparseCore 0:
  9.9 78.8 all-gather.1
  138.4 88.0 reduce-scatter.7
  230.6 90.0 reduce-scatter.5
